TPU v7x, 256 devices: a whole 4x4x8 slice. The times are simulated.
256 devices in a mesh: orb: 16 (over y, x), aux: 16 (over z, core).
Axes of the slice: x: 4, y: 4, z: 8, core: 2. Of those that a mesh axis runs over, the one named last changes fastest.
Arguments:
- b_rows: bfloat16 [4096, 128, 8, 128], P('aux', 'orb'), may hold values from -6 to 6
- col_blocks: int32 [16, 8], P('orb'), may hold values from 0 to 15, all different within a row
- g_occ: bfloat16 [2, 128, 128], P(None, 'orb'), may hold values from -0.5 to 0.5
- occ_live: int32 [2, 16, 16], replicated, may hold values 0 or 1
- g_virt: bfloat16 [2, 16, 128, 128], P(None, 'orb', 'aux'), may hold values from -0.5 to 0.5
- tau_weight: float32 [2], replicated, may hold values from 0.5 to 2
Outputs:
- chi: float32 [256, 4096], P('orb', 'aux')
Inputs may be any that keep to these rules, and one draw needn't show every extreme that they name: `col_blocks`: each row group lists 8 different column blocks, and every column block is listed by some row group.
All inputs are finite; a program needn't handle non-finite values.
Results may differ from a plain program's by a relative error of at most 0.0041.
Values may be sent and summed in bfloat16 or wider, within the bound.
A program may use at most 128 MiB of HBM per device.

v0:
```python
import math
import jax
import jax.numpy as jnp
from jax import lax
from jax.sharding import PartitionSpec as P


def on_device(b_rows, col_blocks, g_occ, occ_live, g_virt, tau_weight):
    orb_count = lax.axis_size("orb")
    aux_dev, rows_dev, slot_count, tile_width = b_rows.shape
    tau_count = g_occ.shape[0]
    picked = (col_blocks[0][:, None] == jnp.arange(orb_count, dtype=jnp.int32)[None, :]).astype(
        jnp.bfloat16
    )
    outgoing = jnp.einsum("prkc,kd->prdc", b_rows, picked)
    occ_full = lax.all_gather(g_occ, "orb", axis=1, tiled=True)
    total_rows = occ_full.shape[1]
    live_mask = jnp.repeat(jnp.repeat(occ_live, rows_dev, axis=1), rows_dev, axis=2).astype(
        jnp.bfloat16
    )
    occ_masked = occ_full * live_mask
    virt_block = lax.all_gather(g_virt, "aux", axis=2, tiled=True)
    col_dense = lax.all_to_all(outgoing, "orb", split_axis=2, concat_axis=1, tiled=True).reshape(
        aux_dev, total_rows, tile_width
    )
    virt_list = []
    for moment in range(tau_count):
        product = jnp.dot(
            col_dense.reshape(aux_dev * total_rows, tile_width),
            virt_block[moment, 0],
            preferred_element_type=jnp.float32,
        )
        virt_list.append(product.astype(jnp.bfloat16).reshape(aux_dev, total_rows, tile_width))
    partial_value = jnp.zeros((aux_dev, aux_dev), jnp.float32)
    for moment in range(tau_count):
        occ_prod = jnp.einsum(
            "mn,qnc->qmc", occ_masked[moment], col_dense, preferred_element_type=jnp.float32
        ).astype(jnp.bfloat16)
        term = jnp.einsum(
            "pmc,qmc->qp", virt_list[moment], occ_prod, preferred_element_type=jnp.float32
        )
        partial_value = partial_value + tau_weight[moment] * term
    partial_value = partial_value * (1.0 / math.sqrt(total_rows * tile_width * orb_count))
    whole_sum = lax.psum(partial_value, "orb")
    share_rows = aux_dev // orb_count
    share = lax.dynamic_slice_in_dim(whole_sum, lax.axis_index("orb") * share_rows, share_rows, 0)
    return share


def solution(mesh):
    in_specs = (
        P("aux", "orb", None, None),
        P("orb", None),
        P(None, "orb", None),
        P(),
        P(None, "orb", "aux", None),
        P(),
    )
    out_specs = P("orb", "aux")
    return jax.shard_map(
        on_device, mesh=mesh, in_specs=in_specs, out_specs=out_specs, check_vma=False
    )
```

profile of v0, /device:TPU:2, one launch (start us, length us, event | category | flops | bytes accessed | tf_op | source)
XLA Modules:
  0.0 368.9 jit_solution(9843376873879229038)
XLA Ops:
  6.5 6.3 %convolution_bitcast_fusion = bf16[256,8,16,128]{3,2,1,0:T(8,128)(2,1)} fusion(bf16[256,8,8,128]{3,2,1,0:T(8,128)(2,1)} %param.6, s32[8]{0:T(128)} %bitcast.83), kind=kOutput, calls=%fused_computation.8 | convolution fusion | flops 67108992 | bytes 12582944 | tf_op jit(solution)/shard_map/prkc,kd->prdc/dot_general | solution.py:15
  12.8 8.8 %copy.23 = bf16[256,8,16,128]{3,1,0,2:T(8,128)(2,1)} copy(bf16[256,8,16,128]{3,2,1,0:T(8,128)(2,1)} %convolution_bitcast_fusion) | data formatting | bytes 16777216 | tf_op jit(solution)/shard_map/prkc,kd->prdc/transpose | solution.py:15
  21.6 0.0 copy-start.1
  21.6 0.0 copy-start.2
  21.6 0.0 copy-start.3
  21.6 0.0 copy-start.4
  21.6 7.6 %all-to-all-start = ((bf16[256,8,16,128]{3,1,0,2:T(8,128)(2,1)}), bf16[256,8,16,128]{3,1,0,2:T(8,128)(2,1)}, u32[]{:S(2)}, u32[]{:S(2)}) async-start(bf16[256,8,16,128]{3,1,0,2:T(8,128)(2,1)} %copy.23), calls=%async_computation | async-start | bytes 16777216 | tf_op jit(solution)/shard_map/all_to_all | solution.py:23
  29.2 0.0 all-reduce.2.cloned.1.call-start
  29.3 0.0 copy-done.1
  29.3 0.1 copy.25
  29.4 0.1 copy.26
  29.5 0.0 copy-done.2
  29.5 137.6 %all_gather.6 = bf16[2,128,128]{2,1,0:T(8,128)(2,1)S(1)} all-gather(bf16[2,8,128]{2,1,0:T(8,128)(2,1)S(1)} %copy-done.2), channel_id=1, replica_groups=mesh['orb'=16,'aux'=16] {'orb'}, dimensions={1}, use_global_device_ids=true | all-gather | bytes 69632 | tf_op jit(solution)/shard_map/all_gather | solution.py:16
  167.1 0.0 copy-done.3
  167.2 20.1 %all_gather.7 = bf16[2,1,128,128]{3,2,1,0:T(8,128)(2,1)S(1)} all-gather(bf16[2,1,8,128]{3,2,1,0:T(8,128)(2,1)S(1)} %copy-done.3), channel_id=1, replica_groups=mesh['orb'=16,'aux'=16] {'aux'}, dimensions={2}, use_global_device_ids=true | all-gather | bytes 69632 | tf_op jit(solution)/shard_map/all_gather | solution.py:22
  187.3 0.0 copy-done.4
  187.3 0.6 fusion.31
  187.9 0.0 all-to-all-done
  187.9 9.0 %copy.34 = bf16[256,8,16,128]{3,1,2,0:T(8,128)(2,1)} copy(bf16[256,8,16,128]{3,1,0,2:T(8,128)(2,1)} %all-to-all-done) | data formatting | bytes 16777216 | tf_op jit(solution)/shard_map/all_to_all | solution.py:23
  196.9 0.0 copy-start
  196.9 9.1 %convolution_convert_fusion = bf16[32768,128]{1,0:T(8,128)(2,1)} fusion(bf16[32768,128]{1,0:T(8,128)(2,1)} %bitcast.78, bf16[2,1,128,128]{3,2,1,0:T(8,128)(2,1)S(1)} %all_gather.7), kind=kOutput, calls=%fused_computation | convolution fusion | flops 1077936128 | bytes 16809984 | tf_op jit(solution)/shard_map/dot_general | solution.py:28
  206.0 0.0 copy-done
  206.0 4.5 %convolution_convert_fusion.1 = bf16[32768,128]{1,0:T(8,128)(2,1)} fusion(bf16[32768,128]{1,0:T(8,128)(2,1)S(1)} %bitcast.80, bf16[2,1,128,128]{3,2,1,0:T(8,128)(2,1)S(1)} %all_gather.7), kind=kOutput, calls=%fused_computation.1 | convolution fusion | flops 1077936128 | bytes 16809984 | tf_op jit(solution)/shard_map/dot_general | solution.py:28
  210.5 11.8 %copy.30 = bf16[256,128,128]{1,0,2:T(8,128)(2,1)} copy(bf16[256,128,128]{2,1,0:T(8,128)(2,1)} %bitcast.82) | data formatting | bytes 16777216 | tf_op jit(solution)/shard_map/reshape | solution.py:33
  222.3 11.8 %copy.27 = bf16[256,128,128]{1,0,2:T(8,128)(2,1)} copy(bf16[256,128,128]{2,1,0:T(8,128)(2,1)} %bitcast.79) | data formatting | bytes 16777216 | tf_op jit(solution)/shard_map/reshape | solution.py:23
  234.1 12.3 %copy.28 = bf16[256,128,128]{1,0,2:T(8,128)(2,1)} copy(bf16[256,128,128]{2,1,0:T(8,128)(2,1)} %bitcast.81) | data formatting | bytes 16777216 | tf_op jit(solution)/shard_map/reshape | solution.py:33
  246.4 11.0 %fusion.16 = f32[256,256]{1,0:T(8,128)S(1)} fusion(bf16[256,128,128]{1,0,2:T(8,128)(2,1)} %copy.30, bf16[256,128,128]{1,0,2:T(8,128)(2,1)} %copy.27, f32[]{:T(128)} %bitcast.18, bf16[2,128,128]{2,1,0:T(8,128)(2,1)S(1)} %mul.25), kind=kOutput, calls=%fused_computation.13 | convolution fusion | flops 3225485312 | bytes 17072132 | tf_op jit(solution)/shard_map/pmc,qmc->qp/dot_general | solution.py:39
  257.5 11.8 %fusion.25 = f32[256,256]{1,0:T(8,128)} fusion(f32[256,256]{1,0:T(8,128)S(1)} %fusion.16, bf16[256,128,128]{1,0,2:T(8,128)(2,1)} %copy.28, bf16[256,128,128]{1,0,2:T(8,128)(2,1)} %copy.27, f32[]{:T(128)} %bitcast, bf16[2,128,128]{2,1,0:T(8,128)(2,1)S(1)} %mul.25), kind=kOutput, calls=%fused_computation.16 | convolution fusion | flops 3225616384 | bytes 17334276 | tf_op jit(solution)/shard_map/pmc,qmc->qp/dot_general | solution.py:39
  269.3 0.0 all-reduce.2.cloned.1.call-update
  269.3 91.4 %all-reduce.2.cloned.1.call-done = f32[256,256]{1,0:T(8,128)} async-done(((f32[256,256]{1,0:T(8,128)}), f32[256,256]{1,0:T(8,128)}) %all-reduce.2.cloned.1.call-update) | async-done | bytes 262160 | tf_op jit(solution)/shard_map/psum | solution.py:44
  360.7 1.3 constant_dynamic-slice_fusion
  (4 shorter events, 0.1 us)
Async XLA Ops:
  21.6 7.7 %copy-start.1 = (s32[2,16,16]{2,1,0:T(8,128)S(1)}, s32[2,16,16]{2,1,0:T(8,128)}, u32[]{:S(2)}) copy-start(s32[2,16,16]{2,1,0:T(8,128)} %param.9) | copy-start | bytes 6148
  21.6 8.0 %copy-start.2 = (bf16[2,8,128]{2,1,0:T(8,128)(2,1)S(1)}, bf16[2,8,128]{2,1,0:T(8,128)(2,1)}, u32[]{:S(2)}) copy-start(bf16[2,8,128]{2,1,0:T(8,128)(2,1)} %param.8) | copy-start | bytes 12292
  21.6 145.6 %copy-start.3 = (bf16[2,1,8,128]{3,2,1,0:T(8,128)(2,1)S(1)}, bf16[2,1,8,128]{3,2,1,0:T(8,128)(2,1)}, u32[]{:S(2)}) copy-start(bf16[2,1,8,128]{3,2,1,0:T(8,128)(2,1)} %param.10) | copy-start | bytes 12292
  21.6 165.7 %copy-start.4 = (f32[2]{0:T(128)S(1)}, f32[2]{0:T(128)}, u32[]{:S(2)}) copy-start(f32[2]{0:T(128)} %param.11) | copy-start | bytes 28
  21.6 166.3 %all-to-all-start = ((bf16[256,8,16,128]{3,1,0,2:T(8,128)(2,1)}), bf16[256,8,16,128]{3,1,0,2:T(8,128)(2,1)}, u32[]{:S(2)}, u32[]{:S(2)}) async-start(bf16[256,8,16,128]{3,1,0,2:T(8,128)(2,1)} %copy.23), calls=%async_computation | async-start | bytes 16777216 | tf_op jit(solution)/shard_map/all_to_all | solution.py:23
  29.2 331.5 %all-reduce.2.cloned.1.call-start = ((), (), s32[]{:S(2)}) async-start(), calls=%async_computation.1 | async-start | bytes 524288 | tf_op jit(solution)/shard_map/psum | solution.py:44
  196.9 9.1 %copy-start = (bf16[256,8,16,128]{3,1,2,0:T(8,128)(2,1)S(1)}, bf16[256,8,16,128]{3,1,2,0:T(8,128)(2,1)}, u32[]{:S(2)}) copy-start(bf16[256,8,16,128]{3,1,2,0:T(8,128)(2,1)} %copy.34) | copy-start | bytes 25165828
Sparse Core Ops, SparseCore 0:
  269.4 91.2 all-reduce.1
where the time goes:
time: 370 us; the launch traced here: 369 us
  blocking collectives  158 us (43%)
  waiting for transfers between devices  91.4 us (25%)
  local copies, waits for them, and re-layouts  55.9 us (15%)
  matrix products  42.7 us (12%)
  between operations  13.5 us (4%)
  starting transfers between devices  7.66 us (2%)
    all_gather x1, blocking collectives, on_device(): occ_full = lax.all_gather(g_occ, 'orb', axis=1, tiled=True)  138 us
    psum x1, waiting for transfers between devices, on_device(): whole_sum = lax.psum(partial_value, 'orb')  91.4 us
    reshape x2, local copies, waits for them, and re-layouts, on_device(): product.astype(jnp.bfloat16).reshape(aux_dev, total_rows, tile_width)  24.1 us
    dot_general x2, matrix products, on_device(): jnp.einsum('pmc,qmc->qp', virt_list[moment], occ_prod, preferred_element_...  22.9 us
    all_gather x1, blocking collectives, on_device(): virt_block = lax.all_gather(g_virt, 'aux', axis=2, tiled=True)  20.1 us
    dot_general x2, matrix products, on_device(): jnp.dot(col_dense.reshape(aux_dev * total_rows, tile_width), virt_block[m...  13.6 us
    reshape x1, local copies, waits for them, and re-layouts, on_device(): lax.all_to_all(outgoing, 'orb', split_axis=2, concat_axis=1, tiled=True)  11.8 us
    all_to_all x1, local copies, waits for them, and re-layouts, on_device(): lax.all_to_all(outgoing, 'orb', split_axis=2, concat_axis=1, tiled=True)  9.03 us
  transfers between devices with their start and end apart: 2, of which 1 were waited for; matrix products, arithmetic and copies ran while one was open for 0% of the time, Pallas kernels for 0%

commit v1 on v0

--- a/solution.py
+++ b/solution.py
@@ -20,9 +20,10 @@
     )
     occ_masked = occ_full * live_mask
     virt_block = lax.all_gather(g_virt, "aux", axis=2, tiled=True)
-    col_dense = lax.all_to_all(outgoing, "orb", split_axis=2, concat_axis=1, tiled=True).reshape(
-        aux_dev, total_rows, tile_width
-    )
+    col_dense = jnp.concatenate(
+        lax.all_to_all(jnp.stack(jnp.split(outgoing, lax.axis_size("orb"), axis=2)), "orb", 0, 0),
+        axis=1,
+    ).reshape(aux_dev, total_rows, tile_width)
     virt_list = []
     for moment in range(tau_count):
         product = jnp.dot(

time: 370 us -> 392 us (1.059)
  local copies, waits for them, and re-layouts: 55.9 us -> 84.5 us
  matrix products: 42.7 us -> 36.2 us
    another operation x0 -> x3, local copies, waits for them, and re-layouts: none -> 20.6 us  [the longest x2 19.6 us: on_device(): col_dense = jnp.concatenate(lax.all_to_all(jnp.stack(jnp.split(outgoing,...]
    unnamed x10 -> x37, local copies, waits for them, and re-layouts: 0.02 us -> 19.8 us
    split x0 -> x1, local copies, waits for them, and re-layouts: none -> 17.9 us  [on_device(): jnp.split(outgoing, lax.axis_size('orb'), axis=2)]
    reshape x1 -> x0, local copies, waits for them, and re-layouts: 11.8 us -> none  [on_device(): lax.all_to_all(outgoing, 'orb', split_axis=2, concat_axis=1, tiled=True)]
    all_to_all x1 -> x0, local copies, waits for them, and re-layouts: 9.03 us -> none  [on_device(): lax.all_to_all(outgoing, 'orb', split_axis=2, concat_axis=1, tiled=True)]
    transpose x1 -> x0, local copies, waits for them, and re-layouts: 8.77 us -> none  [on_device(): outgoing = jnp.einsum('prkc,kd->prdc', b_rows, picked)]
    dot_general x2, matrix products: 13.6 us -> 8.94 us  [on_device(): jnp.dot(col_dense.reshape(aux_dev * total_rows, tile_width), virt_block[m...]
where the time goes in v1:
time: 392 us; the launch traced here: 391 us
  blocking collectives  158 us (40%)
  waiting for transfers between devices  91.4 us (23%)
  local copies, waits for them, and re-layouts  84.5 us (22%)
  matrix products  36.2 us (9%)
  between operations  13.6 us (3%)
  starting transfers between devices  7.66 us (2%)
    all_gather x1, blocking collectives, on_device(): occ_full = lax.all_gather(g_occ, 'orb', axis=1, tiled=True)  138 us
    psum x1, waiting for transfers between devices, on_device(): whole_sum = lax.psum(partial_value, 'orb')  91.4 us
    reshape x2, local copies, waits for them, and re-layouts, on_device(): product.astype(jnp.bfloat16).reshape(aux_dev, total_rows, tile_width)  24 us
    dot_general x2, matrix products, on_device(): jnp.einsum('pmc,qmc->qp', virt_list[moment], occ_prod, preferred_element_...  22.9 us
    all_gather x1, blocking collectives, on_device(): virt_block = lax.all_gather(g_virt, 'aux', axis=2, tiled=True)  20.1 us
    unnamed x37, local copies, waits for them, and re-layouts  19.8 us
    another operation x2, local copies, waits for them, and re-layouts, on_device(): col_dense = jnp.concatenate(lax.all_to_all(jnp.stack(jnp.split(outgoing,...  19.6 us
    split x1, local copies, waits for them, and re-layouts, on_device(): jnp.split(outgoing, lax.axis_size('orb'), axis=2)  17.9 us
  transfers between devices with their start and end apart: 2, of which 1 were waited for; matrix products, arithmetic and copies ran while one was open for 0% of the time, Pallas kernels for 0%

profile of v1, /device:TPU:2, one launch (start us, length us, event | category | flops | bytes accessed | tf_op | source)
XLA Modules:
  0.0 391.2 jit_solution(15709180875748478480)
XLA Ops:
  6.5 4.3 %convolution_bitcast_fusion = bf16[256,8,16,128]{3,2,1,0:T(8,128)(2,1)S(1)} fusion(bf16[256,8,8,128]{3,2,1,0:T(8,128)(2,1)} %param.6, s32[8]{0:T(128)} %bitcast.111), kind=kOutput, calls=%fused_computation.8 | convolution fusion | flops 67108992 | bytes 12582944 | tf_op jit(solution)/shard_map/prkc,kd->prdc/dot_general | solution.py:15
  10.9 17.9 %fusion.31 = (bf16[256,8,1,128]{3,2,1,0:T(2,128)(2,1)S(1)}, bf16[256,8,1,128]{3,2,1,0:T(2,128)(2,1)S(1)}, bf16[256,8,1,128]{3,2,1,0:T(2,128)(2,1)S(1)}, bf16[256...) fusion(bf16[256,8,16,128]{3,2,1,0:T(8,128)(2,1)S(1)} %convoluti, ...), kind=kLoop, calls=%fused_computation.44 | loop fusion | bytes 16777216 | tf_op jit(solution)/shard_map/split | solution.py:24
  28.8 0.0 copy-start.6
  28.9 0.0 copy-start.5
  28.9 0.0 copy-start.4
  28.9 0.0 copy-start.3
  28.9 0.0 copy-start.2
  28.9 0.0 copy-start.1
  28.9 0.0 copy-start
  28.9 2.2 bitcast_dynamic-update-slice_fusion.15
  31.2 2.5 bitcast_dynamic-update-slice_fusion.14
  33.6 2.1 bitcast_dynamic-update-slice_fusion.13
  35.7 2.1 bitcast_dynamic-update-slice_fusion.12
  37.8 2.1 bitcast_dynamic-update-slice_fusion.11
  40.0 0.0 copy-done.6
  40.0 0.9 bitcast_dynamic-update-slice_fusion.10
  40.8 0.0 copy-done.5
  40.8 0.9 bitcast_dynamic-update-slice_fusion.9
  41.7 0.0 copy-done.4
  41.7 0.9 bitcast_dynamic-update-slice_fusion.8
  42.6 0.0 copy-done.3
  42.6 0.9 bitcast_dynamic-update-slice_fusion.7
  43.5 0.0 copy-done.2
  43.5 0.9 bitcast_dynamic-update-slice_fusion.6
  44.3 0.0 copy-done.1
  44.3 0.9 bitcast_dynamic-update-slice_fusion.5
  45.2 0.0 copy-done
  45.2 0.9 bitcast_dynamic-update-slice_fusion.4
  46.1 0.9 bitcast_dynamic-update-slice_fusion.3
  47.0 0.9 bitcast_dynamic-update-slice_fusion.2
  47.9 0.9 bitcast_dynamic-update-slice_fusion.1
  48.7 0.9 bitcast_dynamic-update-slice_fusion
  49.7 0.0 copy-start.7
  49.7 0.0 copy-start.8
  49.7 0.0 copy-start.9
  49.7 0.0 copy-start.10
  49.7 7.6 %all-to-all-start = ((bf16[16,256,8,1,128]{4,2,1,3,0:T(8,128)(2,1)}), bf16[16,256,8,1,128]{4,2,1,3,0:T(8,128)(2,1)}, u32[]{:S(2)}, u32[]{:S(2)}) async-start(bf16[16,256,8,1,128]{4,2,1,3,0:T(8,128)(2,1)} %bitcast_dynamic-update-slice_fusion), calls=%async_computation | async-start | bytes 16777216 | tf_op jit(solution)/shard_map/all_to_all | solution.py:24
  57.3 0.0 all-reduce.2.cloned.1.call-start
  57.3 0.0 copy-done.7
  57.4 0.1 copy.248
  57.5 0.1 copy.249
  57.6 0.0 copy-done.8
  57.6 137.6 %all_gather.6 = bf16[2,128,128]{2,1,0:T(8,128)(2,1)S(1)} all-gather(bf16[2,8,128]{2,1,0:T(8,128)(2,1)S(1)} %copy-done.8), channel_id=1, replica_groups=mesh['orb'=16,'aux'=16] {'orb'}, dimensions={1}, use_global_device_ids=true | all-gather | bytes 69632 | tf_op jit(solution)/shard_map/all_gather | solution.py:16
  195.2 0.0 copy-done.9
  195.2 20.1 %all_gather.7 = bf16[2,1,128,128]{3,2,1,0:T(8,128)(2,1)S(1)} all-gather(bf16[2,1,8,128]{3,2,1,0:T(8,128)(2,1)S(1)} %copy-done.9), channel_id=1, replica_groups=mesh['orb'=16,'aux'=16] {'aux'}, dimensions={2}, use_global_device_ids=true | all-gather | bytes 69632 | tf_op jit(solution)/shard_map/all_gather | solution.py:22
  215.4 0.0 copy-done.10
  215.4 0.7 fusion.32
  216.1 0.0 all-to-all-done
  216.1 7.8 %copy_bitcast_fusion = (bf16[256,128,128]{2,1,0:T(8,128)(2,1)}, bf16[256,16,8,1,128]{4,2,1,0,3:T(8,128)(2,1)S(1)}) fusion(bf16[16,256,8,1,128]{4,2,1,3,0:T(8,128)(2,1)} %all-to-all-done), kind=kLoop, calls=%fused_computation.43 | loop fusion | bytes 25165824 | tf_op jit(solution)/shard_map/reshape;reshape | solution.py:26
  223.9 4.5 %convolution_convert_fusion = bf16[32768,128]{1,0:T(8,128)(2,1)} fusion(bf16[32768,128]{1,0:T(8,128)(2,1)S(1)} %bitcast.107, bf16[2,1,128,128]{3,2,1,0:T(8,128)(2,1)S(1)} %all_gather.7), kind=kOutput, calls=%fused_computation | convolution fusion | flops 1077936128 | bytes 16809984 | tf_op jit(solution)/shard_map/dot_general | solution.py:29
  228.3 4.5 %convolution_convert_fusion.1 = bf16[32768,128]{1,0:T(8,128)(2,1)} fusion(bf16[32768,128]{1,0:T(8,128)(2,1)S(1)} %bitcast.108, bf16[2,1,128,128]{3,2,1,0:T(8,128)(2,1)S(1)} %all_gather.7), kind=kOutput, calls=%fused_computation.1 | convolution fusion | flops 1077936128 | bytes 16809984 | tf_op jit(solution)/shard_map/dot_general | solution.py:29
  232.8 11.8 %copy.254 = bf16[256,128,128]{1,0,2:T(8,128)(2,1)} copy(bf16[256,128,128]{2,1,0:T(8,128)(2,1)} %bitcast.110) | data formatting | bytes 16777216 | tf_op jit(solution)/shard_map/reshape | solution.py:34
  244.6 11.8 %copy.250 = bf16[256,128,128]{1,0,2:T(8,128)(2,1)} copy(bf16[256,128,128]{2,1,0:T(8,128)(2,1)} %get-tuple-element.5) | data formatting | bytes 16777216 | tf_op jit(solution)/shard_map/reshape;reshape | solution.py:26
  256.4 12.2 %copy.252 = bf16[256,128,128]{1,0,2:T(8,128)(2,1)} copy(bf16[256,128,128]{2,1,0:T(8,128)(2,1)} %bitcast.109) | data formatting | bytes 16777216 | tf_op jit(solution)/shard_map/reshape | solution.py:34
  268.6 11.1 %fusion.16 = f32[256,256]{1,0:T(8,128)S(1)} fusion(bf16[256,128,128]{1,0,2:T(8,128)(2,1)} %copy.254, bf16[256,128,128]{1,0,2:T(8,128)(2,1)} %copy.250, f32[]{:T(128)} %bitcast.16, bf16[2,128,128]{2,1,0:T(8,128)(2,1)S(1)} %mul.25), kind=kOutput, calls=%fused_computation.13 | convolution fusion | flops 3225485312 | bytes 17072132 | tf_op jit(solution)/shard_map/pmc,qmc->qp/dot_general | solution.py:40
  279.7 11.8 %fusion.25 = f32[256,256]{1,0:T(8,128)} fusion(f32[256,256]{1,0:T(8,128)S(1)} %fusion.16, bf16[256,128,128]{1,0,2:T(8,128)(2,1)} %copy.252, bf16[256,128,128]{1,0,2:T(8,128)(2,1)} %copy.250, f32[]{:T(128)} %bitcast, bf16[2,128,128]{2,1,0:T(8,128)(2,1)S(1)} %mul.25), kind=kOutput, calls=%fused_computation.16 | convolution fusion | flops 3225616384 | bytes 17334276 | tf_op jit(solution)/shard_map/pmc,qmc->qp/dot_general | solution.py:40
  291.5 0.0 all-reduce.2.cloned.1.call-update
  291.6 91.4 %all-reduce.2.cloned.1.call-done = f32[256,256]{1,0:T(8,128)} async-done(((f32[256,256]{1,0:T(8,128)}), f32[256,256]{1,0:T(8,128)}) %all-reduce.2.cloned.1.call-update) | async-done | bytes 262160 | tf_op jit(solution)/shard_map/psum | solution.py:45
  383.0 1.3 constant_dynamic-slice_fusion
  (4 shorter events, 0.1 us)
Async XLA Ops:
  28.8 11.1 %copy-start.6 = (bf16[256,8,1,128]{3,2,1,0:T(2,128)(2,1)S(1)}, bf16[256,8,1,128]{3,2,1,0:T(2,128)(2,1)}, u32[]{:S(2)}) copy-start(bf16[256,8,1,128]{3,2,1,0:T(2,128)(2,1)} %get-tuple-element.17) | copy-start | bytes 1572868
  28.9 12.0 %copy-start.5 = (bf16[256,8,1,128]{3,2,1,0:T(2,128)(2,1)S(1)}, bf16[256,8,1,128]{3,2,1,0:T(2,128)(2,1)}, u32[]{:S(2)}) copy-start(bf16[256,8,1,128]{3,2,1,0:T(2,128)(2,1)} %get-tuple-element.16) | copy-start | bytes 1572868
  28.9 12.8 %copy-start.4 = (bf16[256,8,1,128]{3,2,1,0:T(2,128)(2,1)S(1)}, bf16[256,8,1,128]{3,2,1,0:T(2,128)(2,1)}, u32[]{:S(2)}) copy-start(bf16[256,8,1,128]{3,2,1,0:T(2,128)(2,1)} %get-tuple-element.15) | copy-start | bytes 1572868
  28.9 13.7 %copy-start.3 = (bf16[256,8,1,128]{3,2,1,0:T(2,128)(2,1)S(1)}, bf16[256,8,1,128]{3,2,1,0:T(2,128)(2,1)}, u32[]{:S(2)}) copy-start(bf16[256,8,1,128]{3,2,1,0:T(2,128)(2,1)} %get-tuple-element.14) | copy-start | bytes 1572868
  28.9 14.6 %copy-start.2 = (bf16[256,8,1,128]{3,2,1,0:T(2,128)(2,1)S(1)}, bf16[256,8,1,128]{3,2,1,0:T(2,128)(2,1)}, u32[]{:S(2)}) copy-start(bf16[256,8,1,128]{3,2,1,0:T(2,128)(2,1)} %get-tuple-element.13) | copy-start | bytes 1572868
  28.9 15.4 %copy-start.1 = (bf16[256,8,1,128]{3,2,1,0:T(2,128)(2,1)S(1)}, bf16[256,8,1,128]{3,2,1,0:T(2,128)(2,1)}, u32[]{:S(2)}) copy-start(bf16[256,8,1,128]{3,2,1,0:T(2,128)(2,1)} %get-tuple-element.12) | copy-start | bytes 1572868
  28.9 16.3 %copy-start = (bf16[256,8,1,128]{3,2,1,0:T(2,128)(2,1)S(1)}, bf16[256,8,1,128]{3,2,1,0:T(2,128)(2,1)}, u32[]{:S(2)}) copy-start(bf16[256,8,1,128]{3,2,1,0:T(2,128)(2,1)} %get-tuple-element.11) | copy-start | bytes 1572868
  49.7 7.7 %copy-start.7 = (s32[2,16,16]{2,1,0:T(8,128)S(1)}, s32[2,16,16]{2,1,0:T(8,128)}, u32[]{:S(2)}) copy-start(s32[2,16,16]{2,1,0:T(8,128)} %param.9) | copy-start | bytes 6148
  49.7 8.0 %copy-start.8 = (bf16[2,8,128]{2,1,0:T(8,128)(2,1)S(1)}, bf16[2,8,128]{2,1,0:T(8,128)(2,1)}, u32[]{:S(2)}) copy-start(bf16[2,8,128]{2,1,0:T(8,128)(2,1)} %param.8) | copy-start | bytes 12292
  49.7 145.6 %copy-start.9 = (bf16[2,1,8,128]{3,2,1,0:T(8,128)(2,1)S(1)}, bf16[2,1,8,128]{3,2,1,0:T(8,128)(2,1)}, u32[]{:S(2)}) copy-start(bf16[2,1,8,128]{3,2,1,0:T(8,128)(2,1)} %param.10) | copy-start | bytes 12292
  49.7 165.7 %copy-start.10 = (f32[2]{0:T(128)S(1)}, f32[2]{0:T(128)}, u32[]{:S(2)}) copy-start(f32[2]{0:T(128)} %param.11) | copy-start | bytes 28
  49.7 166.4 %all-to-all-start = ((bf16[16,256,8,1,128]{4,2,1,3,0:T(8,128)(2,1)}), bf16[16,256,8,1,128]{4,2,1,3,0:T(8,128)(2,1)}, u32[]{:S(2)}, u32[]{:S(2)}) async-start(bf16[16,256,8,1,128]{4,2,1,3,0:T(8,128)(2,1)} %bitcast_dynamic-update-slice_fusion), calls=%async_computation | async-start | bytes 16777216 | tf_op jit(solution)/shard_map/all_to_all | solution.py:24
  57.3 325.7 %all-reduce.2.cloned.1.call-start = ((), (), s32[]{:S(2)}) async-start(), calls=%async_computation.1 | async-start | bytes 524288 | tf_op jit(solution)/shard_map/psum | solution.py:45
Sparse Core Ops, SparseCore 0:
  291.7 91.2 all-reduce.1
